TPU v7x, 32 devices: a whole 2x2x4 slice. The times are simulated.
32 devices in a mesh: dp: 8 (over z, x), grp: 4 (over y, core).
Axes of the slice: x: 2, y: 2, z: 4, core: 2. Of those that a mesh axis runs over, the one named last changes fastest.
Arguments:
- down_in: bfloat16 [96, 32, 32, 160], P(('dp', 'grp')), may hold values from -6 to 6
- right_in: bfloat16 [96, 32, 32, 160], P(('dp', 'grp')), may hold values from -6 to 6
- pixel_mask: int32 [96, 32, 32], P(('dp', 'grp')), may hold values 0 or 1
- down_cot: bfloat16 [96, 32, 32, 160], P(('dp', 'grp')), may hold values from -6 to 6
- right_cot: bfloat16 [96, 32, 32, 160], P(('dp', 'grp')), may hold values from -6 to 6
- v_down1: bfloat16 [2, 1920, 160], P(None, 'dp'), may hold values from -0.125 to 0.125
- v_down2: bfloat16 [2, 1920, 320], P(None, 'dp'), may hold values from -0.125 to 0.125
- v_right1: bfloat16 [2, 1280, 160], P(None, 'dp'), may hold values from -0.15625 to 0.15625
- v_skip: bfloat16 [2, 320, 160], P(None, 'dp'), may hold values from -0.3125 to 0.3125
- v_right2: bfloat16 [2, 1280, 320], P(None, 'dp'), may hold values from -0.15625 to 0.15625
- gains: float32 [2, 1120], replicated, may hold values from 0.1 to 1.9
- biases: float32 [2, 1120], replicated, may hold values from -0.5 to 0.5
Outputs:
- down_out: bfloat16 [96, 32, 32, 160], P(('dp', 'grp'))
- right_out: bfloat16 [96, 32, 32, 160], P(('dp', 'grp'))
- down_grad: float32 [96, 32, 32, 160], P(('dp', 'grp'))
- right_grad: float32 [96, 32, 32, 160], P(('dp', 'grp'))
- grad_down1: float32 [2, 1920, 160], P(None, 'dp')
- grad_down2: float32 [2, 1920, 320], P(None, 'dp')
- grad_right1: float32 [2, 1280, 160], P(None, 'dp')
- grad_skip: float32 [2, 320, 160], P(None, 'dp')
- grad_right2: float32 [2, 1280, 320], P(None, 'dp')
- grad_gains: float32 [2, 1120], replicated
- grad_biases: float32 [2, 1120], replicated
Inputs may be any that keep to these rules, and one draw needn't show every extreme that they name: `pixel_mask`: 1 marks a counted pixel, 0 one that is not.
All inputs are finite; a program needn't handle non-finite values. No bound on the sum of `pixel_mask` on one device may be relied on, other than what follows from the above.
Results may differ from a plain program's by a relative error of at most 0.015.
Values may be sent and summed in bfloat16 or wider, within the bound.
A program may use at most 256 MiB of HBM per device.

v0:
```python
import jax
import jax.numpy as jnp
from jax import lax
from jax.sharding import PartitionSpec as P

LAYERS = 2


def span_list(filters):
    return [
        (0, filters),
        (filters, 3 * filters),
        (3 * filters, 4 * filters),
        (4 * filters, 5 * filters),
        (5 * filters, 7 * filters),
    ]


def tap_offsets(stencil):
    if stencil == "down":
        return [(row_off, col_off) for row_off in range(2) for col_off in range(3)]
    return [(row_off, col_off) for row_off in range(2) for col_off in range(2)]


def side_pad(stencil):
    return 2 if stencil == "down" else 1


def padded_cells(cells, stencil):
    return jnp.pad(cells, ((0, 0), (1, 0), (1, side_pad(stencil) - 1), (0, 0)))


def conv_apply(cells, weight, stencil):
    height, breadth, channels = (cells.shape[1], cells.shape[2], cells.shape[3])
    padded = padded_cells(cells, stencil)
    summed = None
    for tap_num, (row_off, col_off) in enumerate(tap_offsets(stencil)):
        window = padded[:, row_off : row_off + height, col_off : col_off + breadth, :]
        weight_tap = weight[tap_num * channels : (tap_num + 1) * channels]
        contrib = jnp.einsum(
            "bhwc,co->bhwo", window, weight_tap, preferred_element_type=jnp.float32
        )
        summed = contrib if summed is None else summed + contrib
    return summed


def conv_input_grad(grad_out, weight, stencil):
    breadth = grad_out.shape[2]
    offsets = tap_offsets(stencil)
    channels = weight.shape[0] // len(offsets)
    summed = None
    for tap_num, (row_off, col_off) in enumerate(offsets):
        weight_tap = weight[tap_num * channels : (tap_num + 1) * channels]
        contrib = jnp.einsum(
            "bhwo,co->bhwc", grad_out, weight_tap, preferred_element_type=jnp.float32
        )
        placed = jnp.pad(
            contrib,
            ((0, 0), (row_off, 1 - row_off), (col_off, side_pad(stencil) - col_off), (0, 0)),
        )
        summed = placed if summed is None else summed + placed
    return summed[:, 1:, 1 : 1 + breadth, :]


def conv_weight_grad(cells, grad_out, stencil):
    height, breadth = (cells.shape[1], cells.shape[2])
    padded = padded_cells(cells, stencil)
    pieces = []
    for row_off, col_off in tap_offsets(stencil):
        window = padded[:, row_off : row_off + height, col_off : col_off + breadth, :]
        pieces.append(
            jnp.einsum("bhwc,bhwo->co", window, grad_out, preferred_element_type=jnp.float32)
        )
    return jnp.concatenate(pieces, axis=0)


def pair_elu(values):
    return jax.nn.elu(jnp.concatenate([values, -values], axis=-1))


def elu_back(grad, source):
    channels = source.shape[-1]
    upper = jnp.where(source > 0, 1.0, jnp.exp(source))
    lower = jnp.where(source < 0, 1.0, jnp.exp(-source))
    return grad[..., :channels] * upper - grad[..., channels:] * lower


def gate_apply(flow, gate):
    channels = flow.shape[-1]
    return flow + gate[..., :channels] * jax.nn.sigmoid(gate[..., channels:])


def gate_back(grad, gate):
    channels = grad.shape[-1]
    top_half = gate[..., :channels]
    squash = jax.nn.sigmoid(gate[..., channels:])
    return jnp.concatenate(
        [grad * squash, grad * top_half * squash * (1.0 - squash)], axis=-1
    ).astype(jnp.bfloat16)


def prepare(whole, gains, spans):
    scaled = []
    inverse = []
    for full, (start_col, stop_col) in zip(whole, spans):
        values = full.astype(jnp.float32)
        recip = lax.rsqrt(jnp.sum(values * values, axis=1))
        scaled.append(
            (values * (gains[:, start_col:stop_col] * recip)[:, None, :]).astype(jnp.bfloat16)
        )
        inverse.append(recip)
    return (scaled, inverse)


def column_sum(grad):
    return jnp.sum(grad, axis=(0, 1, 2), dtype=jnp.float32)


def on_device(
    down_in,
    right_in,
    pixel_mask,
    down_cot,
    right_cot,
    v_down1,
    v_down2,
    v_right1,
    v_skip,
    v_right2,
    gains,
    biases,
):
    filters = down_in.shape[-1]
    spans = span_list(filters)
    shards = (v_down1, v_down2, v_right1, v_skip, v_right2)
    whole = (
        lax.all_gather(v_down1, "dp", axis=1, tiled=True),
        lax.all_gather(v_down2, "dp", axis=1, tiled=True),
        lax.all_gather(v_right1, "dp", axis=1, tiled=True),
        lax.all_gather(v_skip, "dp", axis=1, tiled=True),
        lax.all_gather(v_right2, "dp", axis=1, tiled=True),
    )
    scaled, inverse = prepare(whole, gains, spans)
    down_flow = down_in.astype(jnp.float32)
    right_flow = right_in.astype(jnp.float32)
    activated = pair_elu(down_flow).astype(jnp.bfloat16)
    kept = []
    for layer_num in range(LAYERS):
        weights = [scaled_now[layer_num] for scaled_now in scaled]
        bias_parts = [biases[layer_num, start_col:stop_col] for start_col, stop_col in spans]
        hidden_down = conv_apply(activated, weights[0], "down") + bias_parts[0]
        act_down = pair_elu(hidden_down).astype(jnp.bfloat16)
        gate_down = conv_apply(act_down, weights[1], "down") + bias_parts[1]
        new_down = gate_apply(down_flow, gate_down)
        new_act = pair_elu(new_down).astype(jnp.bfloat16)
        act_right = pair_elu(right_flow).astype(jnp.bfloat16)
        skip_term = jnp.einsum(
            "bhwk,ko->bhwo", new_act, weights[3], preferred_element_type=jnp.float32
        )
        hidden_right = (
            conv_apply(act_right, weights[2], "right") + skip_term + bias_parts[2] + bias_parts[3]
        )
        act_hidden = pair_elu(hidden_right).astype(jnp.bfloat16)
        gate_right = conv_apply(act_hidden, weights[4], "right") + bias_parts[4]
        new_right = gate_apply(right_flow, gate_right)
        kept.append(
            (
                down_flow,
                activated,
                hidden_down,
                act_down,
                gate_down,
                new_down,
                new_act,
                right_flow,
                act_right,
                hidden_right,
                act_hidden,
                gate_right,
            )
        )
        down_flow, right_flow, activated = (new_down, new_right, new_act)
    down_out = down_flow.astype(jnp.bfloat16)
    right_out = right_flow.astype(jnp.bfloat16)
    whole = (
        lax.all_gather(v_down1, "dp", axis=1, tiled=True),
        lax.all_gather(v_down2, "dp", axis=1, tiled=True),
        lax.all_gather(v_right1, "dp", axis=1, tiled=True),
        lax.all_gather(v_skip, "dp", axis=1, tiled=True),
        lax.all_gather(v_right2, "dp", axis=1, tiled=True),
    )
    scaled, inverse = prepare(whole, gains, spans)
    mask_float = pixel_mask.astype(jnp.float32)[..., None]
    grad_down = down_cot.astype(jnp.float32) * mask_float
    grad_right = right_cot.astype(jnp.float32) * mask_float
    grad_cells = jnp.zeros(grad_down.shape[:-1] + (2 * filters,), jnp.float32)
    layer_grads = [None] * LAYERS
    layer_bias = [None] * LAYERS
    for layer_num in reversed(range(LAYERS)):
        (
            down_flow,
            activated,
            hidden_down,
            act_down,
            gate_down,
            new_down,
            new_act,
            right_flow,
            act_right,
            hidden_right,
            act_hidden,
            gate_right,
        ) = kept[layer_num]
        weights = [scaled_now[layer_num] for scaled_now in scaled]
        grad_gate_right = gate_back(grad_right, gate_right)
        grad_w_right2 = conv_weight_grad(act_hidden, grad_gate_right, "right")
        grad_hid_right = elu_back(
            conv_input_grad(grad_gate_right, weights[4], "right"), hidden_right
        ).astype(jnp.bfloat16)
        grad_w_right1 = conv_weight_grad(act_right, grad_hid_right, "right")
        grad_w_skip = jnp.einsum(
            "bhwc,bhwo->co", new_act, grad_hid_right, preferred_element_type=jnp.float32
        )
        grad_cells = grad_cells + jnp.einsum(
            "bhwo,co->bhwc", grad_hid_right, weights[3], preferred_element_type=jnp.float32
        )
        grad_right = grad_right + elu_back(
            conv_input_grad(grad_hid_right, weights[2], "right"), right_flow
        )
        grad_down = grad_down + elu_back(grad_cells, new_down)
        grad_gate_down = gate_back(grad_down, gate_down)
        grad_w_down2 = conv_weight_grad(act_down, grad_gate_down, "down")
        grad_hid_down = elu_back(
            conv_input_grad(grad_gate_down, weights[1], "down"), hidden_down
        ).astype(jnp.bfloat16)
        grad_w_down1 = conv_weight_grad(activated, grad_hid_down, "down")
        grad_cells = conv_input_grad(grad_hid_down, weights[0], "down")
        layer_grads[layer_num] = (
            grad_w_down1,
            grad_w_down2,
            grad_w_right1,
            grad_w_skip,
            grad_w_right2,
        )
        right_bias = column_sum(grad_hid_right)
        layer_bias[layer_num] = jnp.concatenate(
            [
                column_sum(grad_hid_down),
                column_sum(grad_gate_down),
                right_bias,
                right_bias,
                column_sum(grad_gate_right),
            ]
        )
    down_grad = grad_down + elu_back(grad_cells, kept[0][0])
    local_grads = [
        jnp.stack([layer_grads[layer_num][map_num] for layer_num in range(LAYERS)])
        for map_num in range(5)
    ]
    bias_local = jnp.stack(layer_bias)
    row_sums = (
        lax.psum_scatter(local_grads[0], "dp", scatter_dimension=1, tiled=True),
        lax.psum_scatter(local_grads[1], "dp", scatter_dimension=1, tiled=True),
        lax.psum_scatter(local_grads[2], "dp", scatter_dimension=1, tiled=True),
        lax.psum_scatter(local_grads[3], "dp", scatter_dimension=1, tiled=True),
        lax.psum_scatter(local_grads[4], "dp", scatter_dimension=1, tiled=True),
    )
    group_sums = (
        lax.psum(row_sums[0].astype(jnp.bfloat16), "grp").astype(jnp.float32),
        lax.psum(row_sums[1].astype(jnp.bfloat16), "grp").astype(jnp.float32),
        lax.psum(row_sums[2].astype(jnp.bfloat16), "grp").astype(jnp.float32),
        lax.psum(row_sums[3].astype(jnp.bfloat16), "grp").astype(jnp.float32),
        lax.psum(row_sums[4].astype(jnp.bfloat16), "grp").astype(jnp.float32),
    )
    units = [
        shards[map_num].astype(jnp.float32) * inverse[map_num][:, None, :] for map_num in range(5)
    ]
    bias_sum = lax.psum(bias_local, ("dp", "grp"))
    dots_shard = jnp.concatenate(
        [jnp.sum(units[map_num] * group_sums[map_num], axis=1) for map_num in range(5)], axis=1
    )
    gain_sum = lax.psum(dots_shard, "dp")
    grad_dirs = []
    for map_num, (start_col, stop_col) in enumerate(spans):
        factor = (gains[:, start_col:stop_col] * inverse[map_num])[:, None, :]
        grad_dirs.append(
            factor * (group_sums[map_num] - units[map_num] * gain_sum[:, None, start_col:stop_col])
        )
    return (
        down_out,
        right_out,
        down_grad,
        grad_right,
        grad_dirs[0],
        grad_dirs[1],
        grad_dirs[2],
        grad_dirs[3],
        grad_dirs[4],
        gain_sum,
        bias_sum,
    )


def solution(mesh):
    placed = (
        P(("dp", "grp"), None, None, None),
        P(("dp", "grp"), None, None, None),
        P(("dp", "grp"), None, None),
        P(("dp", "grp"), None, None, None),
        P(("dp", "grp"), None, None, None),
        P(None, "dp", None),
        P(None, "dp", None),
        P(None, "dp", None),
        P(None, "dp", None),
        P(None, "dp", None),
        P(),
        P(),
    )
    return jax.shard_map(
        on_device,
        mesh=mesh,
        in_specs=placed,
        out_specs=(
            P(("dp", "grp"), None, None, None),
            P(("dp", "grp"), None, None, None),
            P(("dp", "grp"), None, None, None),
            P(("dp", "grp"), None, None, None),
            P(None, "dp", None),
            P(None, "dp", None),
            P(None, "dp", None),
            P(None, "dp", None),
            P(None, "dp", None),
            P(),
            P(),
        ),
        check_vma=False,
    )
```

profile of v0, /device:TPU:0, one launch (start us, length us, event | category | flops | bytes accessed | tf_op | source)
XLA Modules:
  0.0 1093.7 jit_solution(6300883025291663017)
XLA Ops:
  24.0 33.5 %all_gather.23 = bf16[2,320,160]{2,0,1:T(2,128)(2,1)S(1)} all-gather(bf16[2,40,160]{2,0,1:T(2,128)(2,1)S(1)} %copy.37), channel_id=1, replica_groups=mesh['dp'=8,'grp'=4] {'dp'}, dimensions={1}, use_global_device_ids=true | all-gather | bytes 230400 | tf_op jit(solution)/shard_map/all_gather | solution.py:140
  57.9 36.9 %all_gather.22 = bf16[2,1280,160]{2,0,1:T(2,128)(2,1)S(1)} all-gather(bf16[2,160,160]{2,0,1:T(2,128)(2,1)S(1)} %copy.35), channel_id=1, replica_groups=mesh['dp'=8,'grp'=4] {'dp'}, dimensions={1}, use_global_device_ids=true | all-gather | bytes 921600 | tf_op jit(solution)/shard_map/all_gather | solution.py:139
  97.0 5.3 fusion.3
  105.7 6.1 copy.33
  140.7 40.0 %all-gather.6.cloned.1.call-done = bf16[2,1920,320]{2,1,0:T(8,128)(2,1)} async-done(((bf16[2,240,320]{2,1,0:T(8,128)(2,1)}), bf16[2,1920,320]{2,1,0:T(8,128)(2,1)}) %all-gather.6.cloned.1.call-update) | async-done | bytes 2457616 | tf_op jit(solution)/shard_map/all_gather | solution.py:138
  201.3 7.9 add_add_fusion.3
  223.7 5.4 fusion.292
  267.7 4.9 add_add_fusion.1
  288.1 9.1 add_add_fusion.2
  300.4 11.1 %convert_reduce_fusion.11 = (u32[3,32,160]{2,1,0:T(8,128)}, u32[3,32,160]{2,1,0:T(8,128)}, f32[3,32,32,160]{3,2,1,0:T(8,128)S(1)}) fusion(f32[160]{0:T(256)S(1)} %bitcast.665, f32[160]{0:T(256)S(1)} %bitcast.664, bf16[2,320,160]{1,2,0:T(8,128)(2,1)S(1)} %fusion.156, f32[3,32,32,160]{3,2,1,0:T(8,128)} %get-tuple-element.73, ...), kind=kOutput, calls=%fused_computation.101 | convolution fusion | flops 326338560 | bytes 15190016 | tf_op jit(solution)/shard_map/bhwk,ko->bhwo/dot_general | solution.py:157
  344.2 11.0 %pad_add_fusion.6 = f32[3,33,33,320]{3,2,1,0:T(8,128)} fusion(f32[3,32,32,320]{3,2,1,0:T(8,128)} %fusion.184, f32[3,32,32,320]{3,2,1,0:T(8,128)} %fusion.183, f32[3,32,32,320]{3,2,1,0:T(8,128)} %fusion.182, f32[3,32,32,320]{3,2,1,0:T(8,128)} %fusion.181), kind=kLoop, calls=%fused_computation.26 | loop fusion | flops 3136320 | bytes 19910400 | tf_op jit(solution)/shard_map/add | solution.py:61
  355.2 6.4 convert_reduce_fusion.12
  383.7 11.1 %pad_add_fusion.4 = f32[3,33,33,320]{3,2,1,0:T(8,128)} fusion(f32[3,32,32,320]{3,2,1,0:T(8,128)} %fusion.207, f32[3,32,32,320]{3,2,1,0:T(8,128)} %fusion.206, f32[3,32,32,320]{3,2,1,0:T(8,128)} %fusion.205, f32[3,32,32,320]{3,2,1,0:T(8,128)} %fusion.204), kind=kLoop, calls=%fused_computation.24 | loop fusion | flops 3136320 | bytes 19910400 | tf_op jit(solution)/shard_map/add | solution.py:61
  394.8 14.6 %multiply_convert_fusion.3 = (bf16[3,32,32,160]{3,2,1,0:T(8,128)(2,1)S(1)}, f32[3,32,32,160]{3,2,1,0:T(8,128)S(1)}, bf16[3,32,32,160]{3,2,1,0:T(8,128)(2,1)}, bf...) fusion(f32[3,32,32,320]{3,2,1,0:T(8,128)} %copy-done.24, f32[3,32,32,160]{3,2,1,0:T(8,128)} %copy-done.39, ...), kind=kLoop, calls=%fused_computation.155 | loop fusion | flops 16220160 | bytes 24588288 | tf_op jit(solution)/shard_map/convert.2
  433.4 11.0 %pad_add_fusion.3 = f32[3,33,33,320]{3,2,1,0:T(8,128)} fusion(f32[3,32,32,320]{3,2,1,0:T(8,128)} %fusion.180, f32[3,32,32,320]{3,2,1,0:T(8,128)} %fusion.179, f32[3,32,32,320]{3,2,1,0:T(8,128)} %fusion.178, f32[3,32,32,320]{3,2,1,0:T(8,128)} %fusion.177), kind=kLoop, calls=%fused_computation.23 | loop fusion | flops 3136320 | bytes 19910400 | tf_op jit(solution)/shard_map/add | solution.py:61
  444.5 6.5 convert_reduce_fusion.14
  475.7 8.8 pad_add_fusion.5
  514.3 12.8 %fusion.20 = f32[3,32,32,320]{3,2,1,0:T(8,128)} fusion(f32[3,32,32,320]{3,2,1,0:T(8,128)} %fusion.198, f32[3,32,32,320]{3,2,1,0:T(8,128)} %fusion.196, f32[3,32,32,320]{3,2,1,0:T(8,128)} %fusion.195, f32[3,32,32,320]{3,2,1,0:T(8,128)} %fusion.194, f32[3,32,32,320]{3,2,1,0:T(8,128)} %fusion.193, f32[3,32,32,320]{3,2,1,0:T(8,128)} %fusion.192, ...), kind=kOutput, calls=%fused_computation.51 | convolution fusion | flops 320471040 | bytes 29220864 | tf_op jit(solution)/shard_map/bhwo,co->bhwc/dot_general | solution.py:224
  580.6 10.7 pad_add_fusion.2
  606.4 6.7 copy.131
  613.0 6.0 reshape.182
  635.2 4.8 concatenate.92
  661.4 9.8 copy.133
  671.2 8.1 reshape.184
  706.4 7.6 copy.43
  716.4 5.7 convolution_bitcast_fusion.4
  724.2 212.3 %all-reduce.56 = (bf16[2,320,160]{2,0,1:T(2,128)(2,1)S(1)}, bf16[2,1280,320]{2,0,1:T(2,128)(2,1)}) all-reduce(f32[2,320,160]{2,0,1:T(2,128)S(1)} %copy.41, f32[2,1280,320]{2,0,1:T(2,128)} %copy.43), channel_id=5, replica_groups=mesh['dp'=8,'grp'=4] {'dp'}, use_global_device_ids=true, to_apply=%region_14.15.clone | all-reduce | flops 921600 | bytes 5529600
  951.0 11.1 %pad_add_fusion = f32[3,33,33,320]{3,2,1,0:T(8,128)} fusion(f32[3,32,32,320]{3,2,1,0:T(8,128)} %fusion.202, f32[3,32,32,320]{3,2,1,0:T(8,128)} %fusion.201, f32[3,32,32,320]{3,2,1,0:T(8,128)} %fusion.200, f32[3,32,32,320]{3,2,1,0:T(8,128)} %fusion.199), kind=kLoop, calls=%fused_computation.20 | loop fusion | flops 3136320 | bytes 19910400 | tf_op jit(solution)/shard_map/add | solution.py:61
  978.9 10.2 pad_add_fusion.1
  1003.6 39.0 %psum.55 = f32[2,1120]{1,0:T(2,128)} all-reduce(f32[2,1120]{1,0:T(2,128)S(1)} %pad_maximum_fusion.9), channel_id=1, replica_groups=mesh['dp'=8,'grp'=4] {'dp','grp'}, use_global_device_ids=true, to_apply=%region_29.30 | all-reduce | flops 2240 | bytes 17920 | tf_op jit(solution)/shard_map/psum | solution.py:278
  1042.7 11.6 %psum.52 = bf16[2,40,160]{2,0,1:T(2,128)(2,1)S(1)} all-reduce(bf16[2,40,160]{2,0,1:T(2,128)(2,1)S(1)} %dynamic-slice_convert_fusion.1), channel_id=1, replica_groups=mesh['dp'=8,'grp'=4] {'grp'}, use_global_device_ids=true, to_apply=%region_15.16 | all-reduce | flops 12800 | bytes 51200 | tf_op jit(solution)/shard_map/psum | solution.py:272
  1059.7 20.5 %psum.54 = f32[2,1120]{1,0:T(2,128)S(1)} all-reduce(f32[2,1120]{1,0:T(2,128)S(1)} %concatenate.97), channel_id=1, replica_groups=mesh['dp'=8,'grp'=4] {'dp'}, use_global_device_ids=true, to_apply=%region_20.21 | all-reduce | flops 2240 | bytes 17920 | tf_op jit(solution)/shard_map/psum | solution.py:282
  (504 shorter events, 469.7 us)
Async XLA Ops:
  7.2 98.6 %all-gather.4.cloned.1.call-start = ((), (), s32[]{:S(2)}) async-start(), calls=%async_computation.3 | async-start | bytes 2211840 | tf_op jit(solution)/shard_map/all_gather | solution.py:137
  9.1 129.5 %all-gather.8.cloned.1.call-start = ((), (), s32[]{:S(2)}) async-start(), calls=%async_computation.5 | async-start | bytes 2211840 | tf_op jit(solution)/shard_map/all_gather | solution.py:141
  9.9 170.8 %all-gather.6.cloned.1.call-start = ((), (), s32[]{:S(2)}) async-start(), calls=%async_computation.4 | async-start | bytes 3317760 | tf_op jit(solution)/shard_map/all_gather | solution.py:138
  11.8 985.0 %reduce-scatter.14.cloned.1.call-start = ((), (), s32[]{:S(2)}) async-start(), calls=%async_computation.8 | async-start | bytes 2211840
  124.6 76.7 %copy-start.18 = (bf16[3,32,32,320]{3,2,1,0:T(8,128)(2,1)}, bf16[3,32,32,320]{3,2,1,0:T(8,128)(2,1)S(1)}, u32[]{:S(2)}) copy-start(bf16[3,32,32,320]{3,2,1,0:T(8,128)(2,1)S(1)} %fusion.5) | copy-start | bytes 5898244
  127.4 250.1 %copy-start.69 = (bf16[2,1280,160]{1,2,0:T(8,128)(2,1)}, bf16[2,1280,160]{1,2,0:T(8,128)(2,1)S(1)}, u32[]{:S(2)}) copy-start(bf16[2,1280,160]{1,2,0:T(8,128)(2,1)S(1)} %fusion.120) | copy-start | bytes 2457604
  183.9 76.4 %copy-start.102 = (f32[2,320]{1,0:T(2,128)}, f32[2,320]{1,0:T(2,128)S(1)}, u32[]{:S(2)}) copy-start(f32[2,320]{1,0:T(2,128)S(1)} %get-tuple-element.97) | copy-start | bytes 7684
  184.5 103.5 %copy-start.47 = (bf16[2,1920,320]{2,1,0:T(8,128)(2,1)}, bf16[2,1920,320]{2,1,0:T(8,128)(2,1)S(1)}, u32[]{:S(2)}) copy-start(bf16[2,1920,320]{2,1,0:T(8,128)(2,1)S(1)} %fusion.1) | copy-start | bytes 7372804
  211.4 85.7 %copy-start.33 = (f32[3,32,32,160]{3,2,1,0:T(8,128)}, f32[3,32,32,160]{3,2,1,0:T(8,128)S(1)}, u32[]{:S(2)}) copy-start(f32[3,32,32,160]{3,2,1,0:T(8,128)S(1)} %get-tuple-element.78) | copy-start | bytes 5898244
  213.6 38.4 %copy-start.5 = (bf16[3,32,32,320]{3,2,1,0:T(8,128)(2,1)}, bf16[3,32,32,320]{3,2,1,0:T(8,128)(2,1)S(1)}, u32[]{:S(2)}) copy-start(bf16[3,32,32,320]{3,2,1,0:T(8,128)(2,1)S(1)} %fusion.7) | copy-start | bytes 5898244
  233.2 54.8 %copy-start.20 = (bf16[3,32,32,320]{3,2,1,0:T(8,128)(2,1)}, bf16[3,32,32,320]{3,2,1,0:T(8,128)(2,1)S(1)}, u32[]{:S(2)}) copy-start(bf16[3,32,32,320]{3,2,1,0:T(8,128)(2,1)S(1)} %fusion.9) | copy-start | bytes 5898244
  274.7 48.0 %copy-start.39 = (f32[3,32,32,160]{3,2,1,0:T(8,128)}, f32[3,32,32,160]{3,2,1,0:T(8,128)S(1)}, u32[]{:S(2)}) copy-start(f32[3,32,32,160]{3,2,1,0:T(8,128)S(1)} %get-tuple-element.76) | copy-start | bytes 5898244
  451.0 63.3 %copy-start.14 = (bf16[3,32,32,160]{3,2,1,0:T(8,128)(2,1)}, bf16[3,32,32,160]{3,2,1,0:T(8,128)(2,1)S(1)}, u32[]{:S(2)}) copy-start(bf16[3,32,32,160]{3,2,1,0:T(8,128)(2,1)S(1)} %get-tuple-element.54) | copy-start | bytes 2949124
  574.4 424.4 %reduce-scatter.10.cloned.1.call-start = ((), (), s32[]{:S(2)}) async-start(), calls=%async_computation.6 | async-start | bytes 3317760
  619.0 381.8 %reduce-scatter.12.cloned.1.call-start = ((), (), s32[]{:S(2)}) async-start(), calls=%async_computation.7 | async-start | bytes 5529600
  682.3 372.2 %all-reduce.55.cloned.1.call-start = ((), (), s32[]{:S(2)}) async-start(), calls=%async_computation.9 | async-start | bytes 1802240 | tf_op jit(solution)/shard_map/psum | solution.py:269
  722.1 216.2 %copy-start.15 = (bf16[3,32,32,160]{3,2,1,0:T(8,128)(2,1)S(1)}, bf16[3,32,32,160]{3,2,1,0:T(8,128)(2,1)}, u32[]{:S(2)}) copy-start(bf16[3,32,32,160]{3,2,1,0:T(8,128)(2,1)} %copy-done.14) | copy-start | bytes 2949124
  722.1 216.2 %copy-start.70 = (bf16[2,1280,160]{1,2,0:T(8,128)(2,1)S(1)}, bf16[2,1280,160]{1,2,0:T(8,128)(2,1)}, u32[]{:S(2)}) copy-start(bf16[2,1280,160]{1,2,0:T(8,128)(2,1)} %copy-done.69) | copy-start | bytes 2457604
  996.7 57.6 %copy-start.93 = (bf16[2,40,160]{2,1,0:T(8,128)(2,1)S(1)}, bf16[2,40,160]{2,1,0:T(8,128)(2,1)}, u32[]{:S(2)}) copy-start(bf16[2,40,160]{2,1,0:T(8,128)(2,1)} %param.20) | copy-start | bytes 76804
  996.7 57.6 %copy-start.112 = (f32[2,160]{1,0:T(2,128)S(1)}, f32[2,160]{1,0:T(2,128)}, u32[]{:S(2)}) copy-start(f32[2,160]{1,0:T(2,128)} %get-tuple-element.106) | copy-start | bytes 3844
  996.7 57.7 %copy-start.78 = (bf16[2,240,160]{1,2,0:T(8,128)(2,1)S(1)}, bf16[2,240,160]{1,2,0:T(8,128)(2,1)}, u32[]{:S(2)}) copy-start(bf16[2,240,160]{1,2,0:T(8,128)(2,1)} %param.17) | copy-start | bytes 460804
  996.7 57.7 %copy-start.113 = (f32[2,160]{1,0:T(2,128)S(1)}, f32[2,160]{1,0:T(2,128)}, u32[]{:S(2)}) copy-start(f32[2,160]{1,0:T(2,128)} %get-tuple-element.104) | copy-start | bytes 3844
  996.7 59.0 %copy-start.76 = (bf16[2,240,320]{1,2,0:T(8,128)(2,1)S(1)}, bf16[2,240,320]{1,2,0:T(8,128)(2,1)}, u32[]{:S(2)}) copy-start(bf16[2,240,320]{1,2,0:T(8,128)(2,1)} %param.18) | copy-start | bytes 921604
  996.7 59.0 %copy-start.107 = (f32[2,320]{1,0:T(2,128)S(1)}, f32[2,320]{1,0:T(2,128)}, u32[]{:S(2)}) copy-start(f32[2,320]{1,0:T(2,128)} %get-tuple-element.102) | copy-start | bytes 7684
  996.7 60.3 %copy-start.77 = (bf16[2,160,320]{2,1,0:T(8,128)(2,1)S(1)}, bf16[2,160,320]{2,1,0:T(8,128)(2,1)}, u32[]{:S(2)}) copy-start(bf16[2,160,320]{2,1,0:T(8,128)(2,1)} %param.21) | copy-start | bytes 614404
  996.8 60.3 %copy-start.104 = (f32[2,320]{1,0:T(2,128)S(1)}, f32[2,320]{1,0:T(2,128)}, u32[]{:S(2)}) copy-start(f32[2,320]{1,0:T(2,128)} %get-tuple-element.103) | copy-start | bytes 7684
  996.8 61.7 %copy-start.79 = (bf16[2,160,160]{1,2,0:T(8,128)(2,1)S(1)}, bf16[2,160,160]{1,2,0:T(8,128)(2,1)}, u32[]{:S(2)}) copy-start(bf16[2,160,160]{1,2,0:T(8,128)(2,1)} %copy.39) | copy-start | bytes 307204
  996.8 61.6 %copy-start.114 = (f32[2,160]{1,0:T(2,128)S(1)}, f32[2,160]{1,0:T(2,128)}, u32[]{:S(2)}) copy-start(f32[2,160]{1,0:T(2,128)} %get-tuple-element.105) | copy-start | bytes 3844
  998.0 82.4 %copy-start.111 = (f32[2,160]{1,0:T(2,128)S(1)}, f32[2,160]{1,0:T(2,128)}, u32[]{:S(2)}) copy-start(f32[2,160]{1,0:T(2,128)} %copy-done.110) | copy-start | bytes 3844
  1000.8 81.6 %copy-start.109 = (f32[2,160]{1,0:T(2,128)S(1)}, f32[2,160]{1,0:T(2,128)}, u32[]{:S(2)}) copy-start(f32[2,160]{1,0:T(2,128)} %copy-done.108) | copy-start | bytes 3844
  1000.8 82.3 %copy-start.116 = (f32[2,160]{1,0:T(2,128)S(1)}, f32[2,160]{1,0:T(2,128)}, u32[]{:S(2)}) copy-start(f32[2,160]{1,0:T(2,128)} %copy-done.115) | copy-start | bytes 3844
  1002.2 81.8 %copy-start.103 = (f32[2,320]{1,0:T(2,128)S(1)}, f32[2,320]{1,0:T(2,128)}, u32[]{:S(2)}) copy-start(f32[2,320]{1,0:T(2,128)} %copy-done.102) | copy-start | bytes 7684
  (107 other events, 776.7 us)
Sparse Core Ops, SparseCore 0:
  10.8 57.5 all-gather.3
  70.6 49.5 all-gather.7
  123.0 57.5 all-gather.5
  574.5 65.3 reduce-scatter.13
  643.7 71.8 reduce-scatter.9
  719.1 166.6 reduce-scatter.11
  1003.7 34.4 all-reduce.54
where the time goes:
time: 1100 us; the launch traced here: 1090 us
  matrix products  364 us (33%)
  blocking collectives  354 us (32%)
  other arithmetic  207 us (19%)
  local copies, waits for them, and re-layouts  110 us (10%)
  waiting for transfers between devices  40.8 us (4%)
  between operations  17.5 us (2%)
    unnamed x1, blocking collectives  212 us
    dot_general x40, matrix products, conv_input_grad(): jnp.einsum('bhwo,co->bhwc', grad_out, weight_tap, preferred_element_type=...  132 us
    dot_general x40, matrix products, conv_apply(): jnp.einsum('bhwc,co->bhwo', window, weight_tap, preferred_element_type=jn...  116 us
    dot_general x40, matrix products, conv_weight_grad(): jnp.einsum('bhwc,bhwo->co', window, grad_out, preferred_element_type=jnp....  76.2 us
    add x7, other arithmetic, conv_input_grad(): summed = placed if summed is None else summed + placed  73.9 us
    unnamed x285, local copies, waits for them, and re-layouts  65.9 us
    all_gather x1, waiting for transfers between devices, on_device(): lax.all_gather(v_down2, 'dp', axis=1, tiled=True)  40 us
    psum x1, blocking collectives, on_device(): bias_sum = lax.psum(bias_local, ('dp', 'grp'))  39 us
  transfers between devices with their start and end apart: 7, of which 1 were waited for; matrix products, arithmetic and copies ran while one was open for 25% of the time, Pallas kernels for 0%

commit v1 on v0

--- a/solution.py
+++ b/solution.py
@@ -275,7 +275,9 @@
     units = [
         shards[map_num].astype(jnp.float32) * inverse[map_num][:, None, :] for map_num in range(5)
     ]
-    bias_sum = lax.psum(bias_local, ("dp", "grp"))
+    bias_sum = bias_local
+    for d in ("grp", "dp"):
+        bias_sum = jax.lax.psum(bias_sum, axis_name=d)
     dots_shard = jnp.concatenate(
         [jnp.sum(units[map_num] * group_sums[map_num], axis=1) for map_num in range(5)], axis=1
     )

time: 1100 us -> 1100 us (level)
  waiting for transfers between devices: 40.8 us -> 57 us
  blocking collectives: 354 us -> 338 us
    psum x1, blocking collectives: 39 us -> 7.7 us  [on_device(): bias_sum = jax.lax.psum(bias_sum, axis_name=d)]
    psum x1, blocking collectives: 20.5 us -> 37.7 us  [on_device(): gain_sum = lax.psum(dots_shard, 'dp')]
    psum x1, waiting for transfers between devices: 0.02 us -> 16.9 us  [on_device(): lax.psum(row_sums[0].astype(jnp.bfloat16), 'grp').astype(jnp.float32)]
  transfers between devices with their start and end apart: 7 -> 7, of which waited for: 1 -> 2; matrix products, arithmetic and copies ran while one was open for 25% -> 25% of each run, Pallas kernels for 0% -> 0%
where the time goes in v1:
time: 1100 us; the launch traced here: 1090 us
  matrix products  363 us (33%)
  blocking collectives  338 us (31%)
  other arithmetic  208 us (19%)
  local copies, waits for them, and re-layouts  110 us (10%)
  waiting for transfers between devices  57 us (5%)
  between operations  17.4 us (2%)
    unnamed x1, blocking collectives  210 us
    dot_general x40, matrix products, conv_input_grad(): jnp.einsum('bhwo,co->bhwc', grad_out, weight_tap, preferred_element_type=...  132 us
    dot_general x40, matrix products, conv_apply(): jnp.einsum('bhwc,co->bhwo', window, weight_tap, preferred_element_type=jn...  116 us
    dot_general x40, matrix products, conv_weight_grad(): jnp.einsum('bhwc,bhwo->co', window, grad_out, preferred_element_type=jnp....  76.2 us
    add x7, other arithmetic, conv_input_grad(): summed = placed if summed is None else summed + placed  73.9 us
    unnamed x285, local copies, waits for them, and re-layouts  65.9 us
    all_gather x1, waiting for transfers between devices, on_device(): lax.all_gather(v_down2, 'dp', axis=1, tiled=True)  39.2 us
    psum x1, blocking collectives, on_device(): gain_sum = lax.psum(dots_shard, 'dp')  37.7 us
  transfers between devices with their start and end apart: 7, of which 2 were waited for; matrix products, arithmetic and copies ran while one was open for 25% of the time, Pallas kernels for 0%

profile of v1, /device:TPU:0, one launch (start us, length us, event | category | flops | bytes accessed | tf_op | source)
XLA Modules:
  0.0 1094.3 jit_solution(13506643902203507373)
XLA Ops:
  24.0 33.5 %all_gather.23 = bf16[2,320,160]{2,0,1:T(2,128)(2,1)S(1)} all-gather(bf16[2,40,160]{2,0,1:T(2,128)(2,1)S(1)} %copy.37), channel_id=1, replica_groups=mesh['dp'=8,'grp'=4] {'dp'}, dimensions={1}, use_global_device_ids=true | all-gather | bytes 230400 | tf_op jit(solution)/shard_map/all_gather | solution.py:140
  57.9 37.5 %all_gather.22 = bf16[2,1280,160]{2,0,1:T(2,128)(2,1)S(1)} all-gather(bf16[2,160,160]{2,0,1:T(2,128)(2,1)S(1)} %copy.35), channel_id=1, replica_groups=mesh['dp'=8,'grp'=4] {'dp'}, dimensions={1}, use_global_device_ids=true | all-gather | bytes 921600 | tf_op jit(solution)/shard_map/all_gather | solution.py:139
  97.4 5.3 fusion.3
  106.2 6.1 copy.33
  141.2 39.2 %all-gather.6.cloned.1.call-done = bf16[2,1920,320]{2,1,0:T(8,128)(2,1)} async-done(((bf16[2,240,320]{2,1,0:T(8,128)(2,1)}), bf16[2,1920,320]{2,1,0:T(8,128)(2,1)}) %all-gather.6.cloned.1.call-update) | async-done | bytes 2457616 | tf_op jit(solution)/shard_map/all_gather | solution.py:138
  201.1 7.9 add_add_fusion.3
  223.4 5.4 fusion.292
  267.4 4.9 add_add_fusion.1
  287.8 9.1 add_add_fusion.2
  300.1 11.1 %convert_reduce_fusion.11 = (u32[3,32,160]{2,1,0:T(8,128)}, u32[3,32,160]{2,1,0:T(8,128)}, f32[3,32,32,160]{3,2,1,0:T(8,128)S(1)}) fusion(f32[160]{0:T(256)S(1)} %bitcast.665, f32[160]{0:T(256)S(1)} %bitcast.664, bf16[2,320,160]{1,2,0:T(8,128)(2,1)S(1)} %fusion.156, f32[3,32,32,160]{3,2,1,0:T(8,128)} %get-tuple-element.75, ...), kind=kOutput, calls=%fused_computation.101 | convolution fusion | flops 326338560 | bytes 15190016 | tf_op jit(solution)/shard_map/bhwk,ko->bhwo/dot_general | solution.py:157
  343.9 11.0 %pad_add_fusion.6 = f32[3,33,33,320]{3,2,1,0:T(8,128)} fusion(f32[3,32,32,320]{3,2,1,0:T(8,128)} %fusion.184, f32[3,32,32,320]{3,2,1,0:T(8,128)} %fusion.183, f32[3,32,32,320]{3,2,1,0:T(8,128)} %fusion.182, f32[3,32,32,320]{3,2,1,0:T(8,128)} %fusion.181), kind=kLoop, calls=%fused_computation.26 | loop fusion | flops 3136320 | bytes 19910400 | tf_op jit(solution)/shard_map/add | solution.py:61
  354.9 6.4 convert_reduce_fusion.12
  383.4 11.1 %pad_add_fusion.4 = f32[3,33,33,320]{3,2,1,0:T(8,128)} fusion(f32[3,32,32,320]{3,2,1,0:T(8,128)} %fusion.207, f32[3,32,32,320]{3,2,1,0:T(8,128)} %fusion.206, f32[3,32,32,320]{3,2,1,0:T(8,128)} %fusion.205, f32[3,32,32,320]{3,2,1,0:T(8,128)} %fusion.204), kind=kLoop, calls=%fused_computation.24 | loop fusion | flops 3136320 | bytes 19910400 | tf_op jit(solution)/shard_map/add | solution.py:61
  394.5 15.0 %multiply_convert_fusion.3 = (bf16[3,32,32,160]{3,2,1,0:T(8,128)(2,1)S(1)}, f32[3,32,32,160]{3,2,1,0:T(8,128)S(1)}, bf16[3,32,32,160]{3,2,1,0:T(8,128)(2,1)}, bf...) fusion(f32[3,32,32,320]{3,2,1,0:T(8,128)} %copy-done.24, f32[3,32,32,160]{3,2,1,0:T(8,128)} %copy-done.39, ...), kind=kLoop, calls=%fused_computation.155 | loop fusion | flops 16220160 | bytes 24588288 | tf_op jit(solution)/shard_map/convert.2
  433.6 11.0 %pad_add_fusion.3 = f32[3,33,33,320]{3,2,1,0:T(8,128)} fusion(f32[3,32,32,320]{3,2,1,0:T(8,128)} %fusion.180, f32[3,32,32,320]{3,2,1,0:T(8,128)} %fusion.179, f32[3,32,32,320]{3,2,1,0:T(8,128)} %fusion.178, f32[3,32,32,320]{3,2,1,0:T(8,128)} %fusion.177), kind=kLoop, calls=%fused_computation.23 | loop fusion | flops 3136320 | bytes 19910400 | tf_op jit(solution)/shard_map/add | solution.py:61
  444.6 6.5 convert_reduce_fusion.14
  475.8 8.8 pad_add_fusion.5
  514.3 12.8 %fusion.20 = f32[3,32,32,320]{3,2,1,0:T(8,128)} fusion(f32[3,32,32,320]{3,2,1,0:T(8,128)} %fusion.198, f32[3,32,32,320]{3,2,1,0:T(8,128)} %fusion.196, f32[3,32,32,320]{3,2,1,0:T(8,128)} %fusion.195, f32[3,32,32,320]{3,2,1,0:T(8,128)} %fusion.194, f32[3,32,32,320]{3,2,1,0:T(8,128)} %fusion.193, f32[3,32,32,320]{3,2,1,0:T(8,128)} %fusion.192, ...), kind=kOutput, calls=%fused_computation.51 | convolution fusion | flops 320471040 | bytes 29220864 | tf_op jit(solution)/shard_map/bhwo,co->bhwc/dot_general | solution.py:224
  580.6 10.7 pad_add_fusion.2
  606.4 6.7 copy.131
  613.1 6.0 reshape.182
  661.3 9.8 copy.133
  671.2 8.1 reshape.184
  706.5 7.6 copy.43
  716.4 5.7 convolution_bitcast_fusion.4
  724.2 210.3 %all-reduce.57 = (bf16[2,320,160]{2,0,1:T(2,128)(2,1)S(1)}, bf16[2,1280,320]{2,0,1:T(2,128)(2,1)}) all-reduce(f32[2,320,160]{2,0,1:T(2,128)S(1)} %copy.41, f32[2,1280,320]{2,0,1:T(2,128)} %copy.43), channel_id=5, replica_groups=mesh['dp'=8,'grp'=4] {'dp'}, use_global_device_ids=true, to_apply=%region_14.15.clone | all-reduce | flops 921600 | bytes 5529600
  949.0 11.1 %pad_add_fusion = f32[3,33,33,320]{3,2,1,0:T(8,128)} fusion(f32[3,32,32,320]{3,2,1,0:T(8,128)} %fusion.202, f32[3,32,32,320]{3,2,1,0:T(8,128)} %fusion.201, f32[3,32,32,320]{3,2,1,0:T(8,128)} %fusion.200, f32[3,32,32,320]{3,2,1,0:T(8,128)} %fusion.199), kind=kLoop, calls=%fused_computation.20 | loop fusion | flops 3136320 | bytes 19910400 | tf_op jit(solution)/shard_map/add | solution.py:61
  976.9 10.2 pad_add_fusion.1
  1001.6 7.7 psum.62
  1009.3 11.5 %psum.59 = bf16[2,40,160]{2,0,1:T(2,128)(2,1)S(1)} all-reduce(bf16[2,40,160]{2,0,1:T(2,128)(2,1)S(1)} %dynamic-slice_convert_fusion.1), channel_id=1, replica_groups=mesh['dp'=8,'grp'=4] {'grp'}, use_global_device_ids=true, to_apply=%region_15.16 | all-reduce | flops 12800 | bytes 51200 | tf_op jit(solution)/shard_map/psum | solution.py:272
  1021.0 16.9 %all-reduce.56.cloned.1.call-done = (bf16[2,240,160]{1,2,0:T(8,128)(2,1)}, bf16[2,240,320]{1,2,0:T(8,128)(2,1)}, bf16[2,160,160]{1,2,0:T(8,128)(2,1)}, bf16[2,160,320]{2,0,1:T(2,128)(2,1)}) async-done(((bf16[2,240,160]{1,2,0:T(8,128)(2,1)}, bf16[2,240,320]{1,2,0:T(8,128)(2,1)}, bf16[2,160,160]{1,2,0:T(8,128)(2,1)}, bf16[2,160,320]{2,0,1:T(2,128)(2,1)}), (bf16[2,240,160]{1,2,0:T(8,128)(2,1)}, ...) | async-done | bytes 768016 | tf_op jit(solution)/shard_map/psum | solution.py:269
  1043.2 37.7 %all-reduce.50 = (f32[2,1120]{1,0:T(2,128)S(1)}, f32[2,1120]{1,0:T(2,128)}) all-reduce(f32[2,1120]{1,0:T(2,128)S(1)} %concatenate.97, f32[2,1120]{1,0:T(2,128)S(1)} %psum.62), channel_id=1, replica_groups=mesh['dp'=8,'grp'=4] {'dp'}, use_global_device_ids=true, to_apply=%region_20.21 | all-reduce | flops 4480 | bytes 35840 | tf_op jit(solution)/shard_map/psum | solution.py:284
  (504 shorter events, 474.3 us)
Async XLA Ops:
  7.2 99.0 %all-gather.4.cloned.1.call-start = ((), (), s32[]{:S(2)}) async-start(), calls=%async_computation.3 | async-start | bytes 2211840 | tf_op jit(solution)/shard_map/all_gather | solution.py:137
  9.1 130.0 %all-gather.8.cloned.1.call-start = ((), (), s32[]{:S(2)}) async-start(), calls=%async_computation.5 | async-start | bytes 2211840 | tf_op jit(solution)/shard_map/all_gather | solution.py:141
  9.9 170.5 %all-gather.6.cloned.1.call-start = ((), (), s32[]{:S(2)}) async-start(), calls=%async_computation.4 | async-start | bytes 3317760 | tf_op jit(solution)/shard_map/all_gather | solution.py:138
  11.8 982.9 %reduce-scatter.14.cloned.1.call-start = ((), (), s32[]{:S(2)}) async-start(), calls=%async_computation.8 | async-start | bytes 2211840
  125.1 76.0 %copy-start.18 = (bf16[3,32,32,320]{3,2,1,0:T(8,128)(2,1)}, bf16[3,32,32,320]{3,2,1,0:T(8,128)(2,1)S(1)}, u32[]{:S(2)}) copy-start(bf16[3,32,32,320]{3,2,1,0:T(8,128)(2,1)S(1)} %fusion.5) | copy-start | bytes 5898244
  127.9 249.3 %copy-start.69 = (bf16[2,1280,160]{1,2,0:T(8,128)(2,1)}, bf16[2,1280,160]{1,2,0:T(8,128)(2,1)S(1)}, u32[]{:S(2)}) copy-start(bf16[2,1280,160]{1,2,0:T(8,128)(2,1)S(1)} %fusion.120) | copy-start | bytes 2457604
  183.7 76.5 %copy-start.101 = (f32[2,320]{1,0:T(2,128)}, f32[2,320]{1,0:T(2,128)S(1)}, u32[]{:S(2)}) copy-start(f32[2,320]{1,0:T(2,128)S(1)} %get-tuple-element.99) | copy-start | bytes 7684
  184.3 103.5 %copy-start.47 = (bf16[2,1920,320]{2,1,0:T(8,128)(2,1)}, bf16[2,1920,320]{2,1,0:T(8,128)(2,1)S(1)}, u32[]{:S(2)}) copy-start(bf16[2,1920,320]{2,1,0:T(8,128)(2,1)S(1)} %fusion.1) | copy-start | bytes 7372804
  211.2 85.7 %copy-start.33 = (f32[3,32,32,160]{3,2,1,0:T(8,128)}, f32[3,32,32,160]{3,2,1,0:T(8,128)S(1)}, u32[]{:S(2)}) copy-start(f32[3,32,32,160]{3,2,1,0:T(8,128)S(1)} %get-tuple-element.80) | copy-start | bytes 5898244
  233.0 54.8 %copy-start.20 = (bf16[3,32,32,320]{3,2,1,0:T(8,128)(2,1)}, bf16[3,32,32,320]{3,2,1,0:T(8,128)(2,1)S(1)}, u32[]{:S(2)}) copy-start(bf16[3,32,32,320]{3,2,1,0:T(8,128)(2,1)S(1)} %fusion.9) | copy-start | bytes 5898244
  274.5 48.0 %copy-start.39 = (f32[3,32,32,160]{3,2,1,0:T(8,128)}, f32[3,32,32,160]{3,2,1,0:T(8,128)S(1)}, u32[]{:S(2)}) copy-start(f32[3,32,32,160]{3,2,1,0:T(8,128)S(1)} %get-tuple-element.78) | copy-start | bytes 5898244
  451.1 63.2 %copy-start.14 = (bf16[3,32,32,160]{3,2,1,0:T(8,128)(2,1)}, bf16[3,32,32,160]{3,2,1,0:T(8,128)(2,1)S(1)}, u32[]{:S(2)}) copy-start(bf16[3,32,32,160]{3,2,1,0:T(8,128)(2,1)S(1)} %get-tuple-element.56) | copy-start | bytes 2949124
  574.5 422.3 %reduce-scatter.10.cloned.1.call-start = ((), (), s32[]{:S(2)}) async-start(), calls=%async_computation.6 | async-start | bytes 3317760
  619.1 379.7 %reduce-scatter.12.cloned.1.call-start = ((), (), s32[]{:S(2)}) async-start(), calls=%async_computation.7 | async-start | bytes 5529600
  682.2 355.7 %all-reduce.56.cloned.1.call-start = ((), (), s32[]{:S(2)}) async-start(), calls=%async_computation.9 | async-start | bytes 1802240 | tf_op jit(solution)/shard_map/psum | solution.py:269
  722.1 214.2 %copy-start.15 = (bf16[3,32,32,160]{3,2,1,0:T(8,128)(2,1)S(1)}, bf16[3,32,32,160]{3,2,1,0:T(8,128)(2,1)}, u32[]{:S(2)}) copy-start(bf16[3,32,32,160]{3,2,1,0:T(8,128)(2,1)} %copy-done.14) | copy-start | bytes 2949124
  722.1 214.2 %copy-start.70 = (bf16[2,1280,160]{1,2,0:T(8,128)(2,1)S(1)}, bf16[2,1280,160]{1,2,0:T(8,128)(2,1)}, u32[]{:S(2)}) copy-start(bf16[2,1280,160]{1,2,0:T(8,128)(2,1)} %copy-done.69) | copy-start | bytes 2457604
  994.7 43.3 %copy-start.112 = (f32[2,160]{1,0:T(2,128)S(1)}, f32[2,160]{1,0:T(2,128)}, u32[]{:S(2)}) copy-start(f32[2,160]{1,0:T(2,128)} %get-tuple-element.106) | copy-start | bytes 3844
  994.7 44.5 %copy-start.76 = (bf16[2,240,320]{1,2,0:T(8,128)(2,1)S(1)}, bf16[2,240,320]{1,2,0:T(8,128)(2,1)}, u32[]{:S(2)}) copy-start(bf16[2,240,320]{1,2,0:T(8,128)(2,1)} %param.18) | copy-start | bytes 921604
  994.7 44.5 %copy-start.106 = (f32[2,320]{1,0:T(2,128)S(1)}, f32[2,320]{1,0:T(2,128)}, u32[]{:S(2)}) copy-start(f32[2,320]{1,0:T(2,128)} %get-tuple-element.104) | copy-start | bytes 7684
  994.7 45.8 %copy-start.77 = (bf16[2,160,320]{2,1,0:T(8,128)(2,1)S(1)}, bf16[2,160,320]{2,1,0:T(8,128)(2,1)}, u32[]{:S(2)}) copy-start(bf16[2,160,320]{2,1,0:T(8,128)(2,1)} %param.21) | copy-start | bytes 614404
  994.7 45.8 %copy-start.103 = (f32[2,320]{1,0:T(2,128)S(1)}, f32[2,320]{1,0:T(2,128)}, u32[]{:S(2)}) copy-start(f32[2,320]{1,0:T(2,128)} %get-tuple-element.105) | copy-start | bytes 7684
  994.7 47.2 %copy-start.79 = (bf16[2,160,160]{1,2,0:T(8,128)(2,1)S(1)}, bf16[2,160,160]{1,2,0:T(8,128)(2,1)}, u32[]{:S(2)}) copy-start(bf16[2,160,160]{1,2,0:T(8,128)(2,1)} %copy.39) | copy-start | bytes 307204
  994.7 47.2 %copy-start.113 = (f32[2,160]{1,0:T(2,128)S(1)}, f32[2,160]{1,0:T(2,128)}, u32[]{:S(2)}) copy-start(f32[2,160]{1,0:T(2,128)} %get-tuple-element.107) | copy-start | bytes 3844
  996.0 85.1 %copy-start.110 = (f32[2,160]{1,0:T(2,128)S(1)}, f32[2,160]{1,0:T(2,128)}, u32[]{:S(2)}) copy-start(f32[2,160]{1,0:T(2,128)} %copy-done.109) | copy-start | bytes 3844
  998.8 84.2 %copy-start.108 = (f32[2,160]{1,0:T(2,128)S(1)}, f32[2,160]{1,0:T(2,128)}, u32[]{:S(2)}) copy-start(f32[2,160]{1,0:T(2,128)} %copy-done.107) | copy-start | bytes 3844
  998.8 85.0 %copy-start.115 = (f32[2,160]{1,0:T(2,128)S(1)}, f32[2,160]{1,0:T(2,128)}, u32[]{:S(2)}) copy-start(f32[2,160]{1,0:T(2,128)} %copy-done.114) | copy-start | bytes 3844
  1000.2 84.5 %copy-start.102 = (f32[2,320]{1,0:T(2,128)S(1)}, f32[2,320]{1,0:T(2,128)}, u32[]{:S(2)}) copy-start(f32[2,320]{1,0:T(2,128)} %copy-done.101) | copy-start | bytes 7684
  1037.9 45.8 %copy-start.84 = (bf16[2,240,160]{1,2,0:T(8,128)(2,1)S(1)}, bf16[2,240,160]{1,2,0:T(8,128)(2,1)}, u32[]{:S(2)}) copy-start(bf16[2,240,160]{1,2,0:T(8,128)(2,1)} %get-tuple-element.49) | copy-start | bytes 460804
  1037.9 46.7 %copy-start.81 = (bf16[2,160,320]{2,0,1:T(2,128)(2,1)S(1)}, bf16[2,160,320]{2,0,1:T(2,128)(2,1)}, u32[]{:S(2)}) copy-start(bf16[2,160,320]{2,0,1:T(2,128)(2,1)} %get-tuple-element.52) | copy-start | bytes 614404
  1038.0 47.9 %copy-start.80 = (bf16[2,240,320]{1,2,0:T(8,128)(2,1)S(1)}, bf16[2,240,320]{1,2,0:T(8,128)(2,1)}, u32[]{:S(2)}) copy-start(bf16[2,240,320]{1,2,0:T(8,128)(2,1)} %get-tuple-element.50) | copy-start | bytes 921604
  1038.0 47.9 %copy-start.105 = (f32[2,320]{1,0:T(2,128)S(1)}, f32[2,320]{1,0:T(2,128)}, u32[]{:S(2)}) copy-start(f32[2,320]{1,0:T(2,128)} %copy-done.104) | copy-start | bytes 7684
  (107 other events, 791.8 us)
Sparse Core Ops, SparseCore 0:
  10.8 57.7 all-gather.3
  70.7 49.2 all-gather.7
  122.9 57.4 all-gather.5
  574.6 65.2 reduce-scatter.13
  643.7 71.3 reduce-scatter.9
  718.6 166.1 reduce-scatter.11
  1001.7 36.2 all-reduce.55
